TPU v7x, 32 devices: a whole 2x2x4 slice. The times are simulated.
32 devices in a mesh: dp: 8 (over y, x, core), head: 4 (over z).
Axes of the slice: x: 2, y: 2, z: 4, core: 2. Of those that a mesh axis runs over, the one named last changes fastest.
Arguments:
- tokens: bfloat16 [16384, 1024], P(('dp', 'head')), may hold values from -6 to 6
- first_values: bfloat16 [16384, 1024], P('dp', 'head'), may hold values from -6 to 6
- mixer_in: float32 [3, 1024, 1024], P(None, 'dp', 'head'), may hold values from -0.1875 to 0.1875
- mixer_out: float32 [1024, 1024], P('head', 'dp'), may hold values from -0.75 to 0.75
- gate_up: float32 [2, 1024, 2816], P(None, 'dp', 'head'), may hold values from -0.1875 to 0.1875
- down_weight: float32 [2816, 1024], P('head', 'dp'), may hold values from -0.109375 to 0.109375
- norm_gains: float32 [2, 1024], P(None, 'dp'), may hold values from 0.5 to 1.5
- lengths: int32 [8], P('dp'), may hold values from 128 to 2048, as said below
- cotangent: bfloat16 [16384, 1024], P(('dp', 'head')), may hold values from -6 to 6
Outputs:
- block_out: bfloat16 [16384, 1024], P(('dp', 'head'))
- tokens_grad: float32 [16384, 1024], P(('dp', 'head'))
- first_grad: float32 [16384, 1024], P('dp', 'head')
- mixer_in_grad: float32 [3, 1024, 1024], P(None, 'dp', 'head')
- mixer_out_grad: float32 [1024, 1024], P('head', 'dp')
- gate_up_grad: float32 [2, 1024, 2816], P(None, 'dp', 'head')
- down_grad: float32 [2816, 1024], P('head', 'dp')
- gains_grad: float32 [2, 1024], P(None, 'dp')
Inputs may be any that keep to these rules, and one draw needn't show every extreme that they name: `lengths`: positions from a sequence's length on are padding; some sequence has exactly 2048 real tokens in every draw.
All inputs are finite; a program needn't handle non-finite values.
Results may differ from a plain program's by a relative error of at most 0.013.
The roundings to bfloat16 on the way count: a program that leaves them out, or rounds other values in their place, can miss the bound.
Values may be sent and summed in bfloat16 or wider, within the bound.
No kernel may reach another device: no remote copies, remote signals or barrier semaphores. Data moves between devices by JAX's collectives and lax.ppermute only.
A program may use at most 128 MiB of HBM per device.

v0:
```python
import jax
import jax.numpy as jnp
from jax import lax
from jax.sharding import PartitionSpec as P

HDIM = 64
SEQ = 2048
epsilon = 1e-05
far_below = -1e30
rope_base = 10000.0


def rope_tables(width):
    half = width // 2
    rates = rope_base ** (-jnp.arange(half, dtype=jnp.float32) * 2.0 / width)
    angles = jnp.arange(SEQ, dtype=jnp.float32)[:, None] * rates[None, :]
    return (jnp.cos(angles)[:, None, :], jnp.sin(angles)[:, None, :])


def rotate(field, cosine, sine, direction):
    half = field.shape[-1] // 2
    first = field[..., :half]
    second = field[..., half:]
    return jnp.concatenate(
        [first * cosine - direction * second * sine, second * cosine + direction * first * sine],
        axis=-1,
    )


def rms_parts(field, gain):
    factor = lax.rsqrt(jnp.mean(field * field, axis=-1, keepdims=True) + epsilon)
    unit = field * factor
    return (unit * gain, unit, factor)


def rms_back(normed_grad, unit, factor, gain):
    scaled = normed_grad * gain
    field_grad = factor * (scaled - unit * jnp.mean(scaled * unit, axis=-1, keepdims=True))
    return (field_grad, jnp.sum(normed_grad * unit, axis=0))


def to_items(rows, seqs_here, heads_here):
    return (
        rows.reshape(seqs_here, SEQ, heads_here, HDIM)
        .transpose(0, 2, 1, 3)
        .reshape(seqs_here * heads_here, SEQ, HDIM)
    )


def from_items(items, seqs_here, heads_here):
    return (
        items.reshape(seqs_here, heads_here, SEQ, HDIM)
        .transpose(0, 2, 1, 3)
        .reshape(seqs_here * SEQ, heads_here * HDIM)
    )


def block_scores(query_block, keys, rows, length):
    places = jnp.arange(SEQ)
    raw = jnp.einsum("qe,ke->qk", query_block, keys, preferred_element_type=jnp.float32)
    allowed = (places[None, :] <= rows[:, None]) & (places[None, :] < length)
    return jnp.where(allowed, raw * HDIM ** (-0.5), far_below)


def attend_item(item):
    query, keys, values, length = item
    block = min(512, SEQ)

    def one_block(number):
        start = number * block
        query_block = lax.dynamic_slice_in_dim(query, start, block, 0)
        rows = start + jnp.arange(block)
        scores = block_scores(query_block, keys, rows, length)
        peak = jnp.max(scores, axis=-1, keepdims=True)
        powers = jnp.exp(scores - peak)
        total = jnp.sum(powers, axis=-1, keepdims=True)
        probs = (powers / total).astype(jnp.bfloat16)
        result = (
            jnp.dot(probs, values, preferred_element_type=jnp.float32) * (rows < length)[:, None]
        )
        return (result.astype(jnp.bfloat16), (peak + jnp.log(total))[:, 0])

    results, log_total = lax.map(one_block, jnp.arange(SEQ // block))
    return (results.reshape(SEQ, HDIM), log_total.reshape(SEQ))


def attend_back(item):
    query, keys, values, length, log_total, out_grad = item
    block = min(512, SEQ)

    def one_block(carry, number):
        keys_grad, values_grad = carry
        start = number * block
        query_block = lax.dynamic_slice_in_dim(query, start, block, 0)
        grad_block = lax.dynamic_slice_in_dim(out_grad, start, block, 0)
        total_block = lax.dynamic_slice_in_dim(log_total, start, block, 0)
        rows = start + jnp.arange(block)
        scores = block_scores(query_block, keys, rows, length)
        probs = jnp.exp(scores - total_block[:, None])
        values_grad = values_grad + jnp.einsum(
            "qk,qe->ke", probs.astype(jnp.bfloat16), grad_block, preferred_element_type=jnp.float32
        )
        prob_grad = jnp.einsum("qe,ke->qk", grad_block, values, preferred_element_type=jnp.float32)
        offset = jnp.sum(prob_grad * probs, axis=-1, keepdims=True)
        raw_grad = (probs * (prob_grad - offset) * HDIM ** (-0.5)).astype(jnp.bfloat16)
        query_grad = jnp.dot(raw_grad, keys, preferred_element_type=jnp.float32)
        keys_grad = keys_grad + jnp.einsum(
            "qk,qe->ke", raw_grad, query_block, preferred_element_type=jnp.float32
        )
        return ((keys_grad, values_grad), query_grad)

    empty = jnp.zeros((SEQ, HDIM), jnp.float32)
    (keys_grad, values_grad), query_grads = lax.scan(
        one_block, (empty, empty), jnp.arange(SEQ // block)
    )
    return (query_grads.reshape(SEQ, HDIM), keys_grad, values_grad)


def shards(
    tokens, first_values, mixer_in, mixer_out, gate_up, down_weight, norm_gains, lengths, cotangent
):
    seqs_here = lengths.shape[0]
    group_rows = seqs_here * SEQ
    heads_here = mixer_in.shape[2] // HDIM
    cosine, sine = rope_tables(HDIM)
    places = jnp.arange(SEQ)
    valid_rows = (places[None, :] < lengths[:, None]).astype(jnp.float32).reshape(group_rows)
    head_lengths = jnp.repeat(lengths, heads_here)
    qkv_low = mixer_in.astype(jnp.bfloat16)
    proj_low = mixer_out.astype(jnp.bfloat16)
    gates_low = gate_up.astype(jnp.bfloat16)
    down_low = down_weight.astype(jnp.bfloat16)
    gain_low = norm_gains.astype(jnp.bfloat16)
    full = (
        lax.all_gather(qkv_low, "dp", axis=1, tiled=True),
        lax.all_gather(proj_low, "dp", axis=1, tiled=True),
        lax.all_gather(gates_low, "dp", axis=1, tiled=True),
        lax.all_gather(down_low, "dp", axis=1, tiled=True),
        lax.all_gather(gain_low, "dp", axis=1, tiled=True),
    )
    qkv_full, proj_full, gates_full, down_full, gain_full = full
    gain_first = gain_full[0].astype(jnp.float32)
    gain_second = gain_full[1].astype(jnp.float32)
    token_rows = tokens.astype(jnp.float32)
    normed_a, unit_a, factor_a = rms_parts(token_rows, gain_first)
    mixer_rows = lax.all_gather(normed_a.astype(jnp.bfloat16), "head", axis=0, tiled=True)
    mixed = jnp.einsum("td,kdc->ktc", mixer_rows, qkv_full, preferred_element_type=jnp.float32)
    shape_four = (seqs_here, SEQ, heads_here, HDIM)
    query = rotate(mixed[0].reshape(shape_four), cosine, sine, 1.0).astype(jnp.bfloat16)
    keys = rotate(mixed[1].reshape(shape_four), cosine, sine, 1.0).astype(jnp.bfloat16)
    values = (0.5 * mixed[2] + 0.5 * first_values.astype(jnp.float32)).astype(jnp.bfloat16)
    query_items = query.transpose(0, 2, 1, 3).reshape(seqs_here * heads_here, SEQ, HDIM)
    keys_items = keys.transpose(0, 2, 1, 3).reshape(seqs_here * heads_here, SEQ, HDIM)
    values_items = to_items(values, seqs_here, heads_here)
    attended_items, log_total = lax.map(
        attend_item, (query_items, keys_items, values_items, head_lengths)
    )
    attended = from_items(attended_items, seqs_here, heads_here)
    piece = attended
    branch_a = lax.psum_scatter(
        jnp.dot(piece, proj_full, preferred_element_type=jnp.float32),
        "head",
        scatter_dimension=0,
        tiled=True,
    )
    hidden_state = token_rows + branch_a
    normed_b, unit_b, factor_b = rms_parts(hidden_state, gain_second)
    feed_rows = lax.all_gather(normed_b.astype(jnp.bfloat16), "head", axis=0, tiled=True)
    gated = jnp.einsum("td,kdf->ktf", feed_rows, gates_full, preferred_element_type=jnp.float32)
    gate = gated[0]
    upward = gated[1]
    sigmoid_gate = jax.nn.sigmoid(gate)
    silu_gate = gate * sigmoid_gate
    inner = (silu_gate * upward).astype(jnp.bfloat16)
    piece = inner
    branch_b = lax.psum_scatter(
        jnp.dot(piece, down_full, preferred_element_type=jnp.float32).astype(jnp.bfloat16),
        "head",
        scatter_dimension=0,
        tiled=True,
    ).astype(jnp.float32)
    block_out = (hidden_state + branch_b).astype(jnp.bfloat16)
    back_full = (
        lax.all_gather(qkv_low, "dp", axis=1, tiled=True),
        lax.all_gather(proj_low, "dp", axis=1, tiled=True),
        lax.all_gather(gates_low, "dp", axis=1, tiled=True),
        lax.all_gather(down_low, "dp", axis=1, tiled=True),
        lax.all_gather(gain_low, "dp", axis=1, tiled=True),
    )
    qkv_back, proj_back, gates_back, down_back, gain_back = back_full
    piece = lax.all_gather(cotangent, "head", axis=0, tiled=True)
    down_sum = jnp.einsum("tf,td->fd", inner, piece, preferred_element_type=jnp.float32)
    rows_grad = jnp.einsum("td,fd->tf", piece, down_back, preferred_element_type=jnp.float32)
    inner_grad = rows_grad
    gate_grad = inner_grad * upward * sigmoid_gate * (1.0 + gate * (1.0 - sigmoid_gate))
    mlp_grad = jnp.stack([gate_grad, inner_grad * silu_gate]).astype(jnp.bfloat16)
    gates_part = jnp.einsum("td,ktf->kdf", feed_rows, mlp_grad, preferred_element_type=jnp.float32)
    piece = mlp_grad
    normed_b_grad = lax.psum_scatter(
        jnp.einsum("ktf,kdf->td", piece, gates_back, preferred_element_type=jnp.float32),
        "head",
        scatter_dimension=0,
        tiled=True,
    )
    state_part, gain_b_grad = rms_back(
        normed_b_grad, unit_b, factor_b, gain_back[1].astype(jnp.float32)
    )
    state_grad = cotangent.astype(jnp.float32) + state_part
    branch_grad = state_grad.astype(jnp.bfloat16)
    piece = lax.all_gather(branch_grad, "head", axis=0, tiled=True)
    proj_sum = jnp.einsum("tc,td->cd", attended, piece, preferred_element_type=jnp.float32)
    rows_grad = jnp.einsum("td,cd->tc", piece, proj_back, preferred_element_type=jnp.float32)
    attended_grad = rows_grad
    attended_grad = (valid_rows[:, None] * attended_grad).astype(jnp.bfloat16)
    grad_items = to_items(attended_grad, seqs_here, heads_here)
    query_grad, keys_grad, values_grad = lax.map(
        attend_back, (query_items, keys_items, values_items, head_lengths, log_total, grad_items)
    )
    values_mix_grad = from_items(values_grad, seqs_here, heads_here)
    first_grad = 0.5 * values_mix_grad
    query_rows = query_grad.reshape(seqs_here, heads_here, SEQ, HDIM).transpose(0, 2, 1, 3)
    keys_rows = keys_grad.reshape(seqs_here, heads_here, SEQ, HDIM).transpose(0, 2, 1, 3)
    query_back = rotate(query_rows, cosine, sine, -1.0).reshape(group_rows, heads_here * HDIM)
    keys_back = rotate(keys_rows, cosine, sine, -1.0).reshape(group_rows, heads_here * HDIM)
    mixed_grad = jnp.stack([query_back, keys_back, 0.5 * values_mix_grad]).astype(jnp.bfloat16)
    qkv_part = jnp.einsum("td,ktc->kdc", mixer_rows, mixed_grad, preferred_element_type=jnp.float32)
    piece = mixed_grad
    normed_a_grad = lax.psum_scatter(
        jnp.einsum("ktc,kdc->td", piece, qkv_back, preferred_element_type=jnp.float32).astype(
            jnp.bfloat16
        ),
        "head",
        scatter_dimension=0,
        tiled=True,
    ).astype(jnp.float32)
    token_part, gain_a_grad = rms_back(
        normed_a_grad, unit_a, factor_a, gain_back[0].astype(jnp.float32)
    )
    tokens_grad = state_grad + token_part
    gain_grads = jnp.stack([gain_a_grad, gain_b_grad])
    summed = (
        lax.psum_scatter(qkv_part, "dp", scatter_dimension=1, tiled=True),
        lax.psum_scatter(proj_sum, "dp", scatter_dimension=1, tiled=True),
        lax.psum_scatter(gates_part, "dp", scatter_dimension=1, tiled=True),
        lax.psum_scatter(down_sum, "dp", scatter_dimension=1, tiled=True),
        lax.psum_scatter(gain_grads, "dp", scatter_dimension=1, tiled=True),
    )
    gains_grad = lax.psum(summed[4], "head")
    return (
        block_out,
        tokens_grad,
        first_grad,
        summed[0],
        summed[1],
        summed[2],
        summed[3],
        gains_grad,
    )


def solution(mesh):
    return jax.shard_map(
        shards,
        mesh=mesh,
        in_specs=(
            P(("dp", "head"), None),
            P("dp", "head"),
            P(None, "dp", "head"),
            P("head", "dp"),
            P(None, "dp", "head"),
            P("head", "dp"),
            P(None, "dp"),
            P("dp"),
            P(("dp", "head"), None),
        ),
        out_specs=(
            P(("dp", "head"), None),
            P(("dp", "head"), None),
            P("dp", "head"),
            P(None, "dp", "head"),
            P("head", "dp"),
            P(None, "dp", "head"),
            P("head", "dp"),
            P(None, "dp"),
        ),
        check_vma=False,
    )
```

profile of v0, /device:TPU:0, one launch (start us, length us, event | category | flops | bytes accessed | tf_op | source)
XLA Modules:
  0.0 1471.1 jit_solution(9712456741320512277)
XLA Ops:
  7.2 1.9 copy.60
  9.9 10.2 all_gather.32
  25.0 12.0 all_gather.35
  39.8 83.2 %all-gather.8.cloned.1.call-done = bf16[2048,1024]{1,0:T(8,128)(2,1)} async-done(((bf16[512,1024]{1,0:T(8,128)(2,1)}), bf16[2048,1024]{1,0:T(8,128)(2,1)}) %all-gather.8.cloned.1.call-update) | async-done | bytes 4194320 | tf_op jit(solution)/shard_map/all_gather | solution.py:146
  123.0 5.7 fusion.29
  135.0 127.7 %while.54 = (s32[]{:T(128)}, bf16[4,2048,64]{1,2,0:T(8,128)(2,1)}, f32[4,2048]{1,0:T(4,128)S(1)}, bf16[4,2048,64]{2,1,0:T(8,128)(2,1)}, bf16[4,2048,64]{2,1,0:T(...) while((s32[]{:T(128)}, bf16[4,2048,64]{1,2,0:T(8,128)(2,1)}, ...), condition=%wide.region_6.7_spmd, body=%wide.region_1.6_spmd.sunk | while | flops 278990336 | bytes 16777708 | solution.py:155
  138.6 27.0 %while.57 = (s32[]{:T(128)}, bf16[4,512,64]{1,2,0:T(8,128)(2,1)S(1)}, f32[4,512]{1,0:T(4,128)S(1)}, s32[4]{0:T(128)S(1)}, s32[]{:T(128)}, /*index=5*/bf16[2048,6...) while((s32[]{:T(128)}, ...), condition=%wide.region_5.5_spmd, body=%wide.region_2.4_spmd.sunk | while | flops 278990336 | bytes 13598931 | solution.py:83
  141.2 2.3 fusion.119
  147.9 2.3 fusion.119
  154.6 2.3 fusion.119
  161.4 2.3 fusion.119
  170.5 27.0 %while.57 = (s32[]{:T(128)}, bf16[4,512,64]{1,2,0:T(8,128)(2,1)S(1)}, f32[4,512]{1,0:T(4,128)S(1)}, s32[4]{0:T(128)S(1)}, s32[]{:T(128)}, /*index=5*/bf16[2048,6...) while((s32[]{:T(128)}, ...), condition=%wide.region_5.5_spmd, body=%wide.region_2.4_spmd.sunk | while | flops 278990336 | bytes 13598931 | solution.py:83
  173.1 2.3 fusion.119
  179.8 2.3 fusion.119
  186.6 2.3 fusion.119
  193.3 2.3 fusion.119
  202.4 27.0 %while.57 = (s32[]{:T(128)}, bf16[4,512,64]{1,2,0:T(8,128)(2,1)S(1)}, f32[4,512]{1,0:T(4,128)S(1)}, s32[4]{0:T(128)S(1)}, s32[]{:T(128)}, /*index=5*/bf16[2048,6...) while((s32[]{:T(128)}, ...), condition=%wide.region_5.5_spmd, body=%wide.region_2.4_spmd.sunk | while | flops 278990336 | bytes 13598931 | solution.py:83
  205.0 2.3 fusion.119
  211.7 2.3 fusion.119
  218.5 2.3 fusion.119
  225.2 2.3 fusion.119
  234.3 27.0 %while.57 = (s32[]{:T(128)}, bf16[4,512,64]{1,2,0:T(8,128)(2,1)S(1)}, f32[4,512]{1,0:T(4,128)S(1)}, s32[4]{0:T(128)S(1)}, s32[]{:T(128)}, /*index=5*/bf16[2048,6...) while((s32[]{:T(128)}, ...), condition=%wide.region_5.5_spmd, body=%wide.region_2.4_spmd.sunk | while | flops 278990336 | bytes 13598931 | solution.py:83
  236.9 2.3 fusion.119
  243.7 2.3 fusion.119
  250.4 2.3 fusion.119
  257.2 2.3 fusion.119
  262.7 6.7 fusion.66
  271.4 141.2 %reduce-scatter.12.cloned.1.call-done = f32[512,1024]{1,0:T(8,128)} async-done(((f32[2048,1024]{1,0:T(8,128)}), f32[512,1024]{1,0:T(8,128)}) %reduce-scatter.12.cloned.1.call-update) | async-done | bytes 2097168 | tf_op jit(solution)/shard_map/reduce_scatter | solution.py:160
  412.6 1.9 multiply_reduce_fusion.3
  417.9 29.4 %all-gather.14.cloned.1.call-done = bf16[2,1024,704]{1,2,0:T(8,128)(2,1)} async-done(((bf16[2,128,704]{1,2,0:T(8,128)(2,1)}), bf16[2,1024,704]{1,2,0:T(8,128)(2,1)}) %all-gather.14.cloned.1.call-update) | async-done | bytes 2883600 | tf_op jit(solution)/shard_map/all_gather | solution.py:137
  447.3 82.8 %all-gather.12.cloned.1.call-done = bf16[2048,1024]{1,0:T(8,128)(2,1)} async-done(((bf16[512,1024]{1,0:T(8,128)(2,1)}), bf16[2048,1024]{1,0:T(8,128)(2,1)}) %all-gather.12.cloned.1.call-update) | async-done | bytes 4194320 | tf_op jit(solution)/shard_map/all_gather | solution.py:168
  530.1 11.5 convolution_bitcast_fusion.1
  541.6 14.7 all-gather.16.cloned.1.call-done
  556.2 82.4 %all-gather.18.cloned.1.call-done = bf16[2048,1024]{1,0:T(8,128)(2,1)} async-done(((bf16[512,1024]{1,0:T(8,128)(2,1)}), bf16[2048,1024]{1,0:T(8,128)(2,1)}) %all-gather.18.cloned.1.call-update) | async-done | bytes 4194320 | tf_op jit(solution)/shard_map/all_gather | solution.py:191
  638.6 11.3 fusion.37
  652.5 9.0 convolution_bitcast_fusion.2
  661.5 143.1 %reduce-scatter.16.cloned.1.call-done = f32[512,1024]{1,0:T(8,128)} async-done(((f32[2048,1024]{1,0:T(8,128)}), f32[512,1024]{1,0:T(8,128)}) %reduce-scatter.16.cloned.1.call-update) | async-done | bytes 2097168 | tf_op jit(solution)/shard_map/reduce_scatter | solution.py:199
  804.6 2.9 multiply_reduce_fusion.1
  809.5 81.4 %all-gather.20.cloned.1.call-done = bf16[2048,1024]{1,0:T(8,128)(2,1)} async-done(((bf16[512,1024]{1,0:T(8,128)(2,1)}), bf16[2048,1024]{1,0:T(8,128)(2,1)}) %all-gather.20.cloned.1.call-update) | async-done | bytes 4194320 | tf_op jit(solution)/shard_map/all_gather | solution.py:210
  890.9 3.6 fusion.38
  896.3 154.4 %while.56 = (s32[]{:T(128)}, f32[4,2048,64]{1,2,0:T(8,128)}, f32[4,2048,64]{1,2,0:T(8,128)}, f32[4,2048,64]{1,2,0:T(8,128)}, bf16[4,2048,64]{2,1,0:T(8,128)(2,1)...) while((s32[]{:T(128)}, f32[4,2048,64]{1,2,0:T(8,128)}, ...), condition=%wide.region_16.17_spmd, body=%wide.region_12.16_spmd.sunk | while | flops 684197888 | bytes 42895948 | solution.py:216
  901.3 30.0 %while.58 = (s32[]{:T(128)}, f32[2048,64]{0,1:T(8,128)S(1)}, f32[2048,64]{0,1:T(8,128)S(1)}, f32[4,512,64]{1,2,0:T(8,128)}, s32[4]{0:T(128)S(1)}, /*index=5*/s32...) while((s32[]{:T(128)}, f32[2048,64]{0,1:T(8,128)S(1)}, ...), condition=%wide.region_15.15_spmd.clone, body=%wide.region_13.14_spmd.clone.sunk | while | flops 684197888 | bytes 35539192 | solution.py:113
  939.9 30.0 %while.58 = (s32[]{:T(128)}, f32[2048,64]{0,1:T(8,128)S(1)}, f32[2048,64]{0,1:T(8,128)S(1)}, f32[4,512,64]{1,2,0:T(8,128)}, s32[4]{0:T(128)S(1)}, /*index=5*/s32...) while((s32[]{:T(128)}, f32[2048,64]{0,1:T(8,128)S(1)}, ...), condition=%wide.region_15.15_spmd.clone, body=%wide.region_13.14_spmd.clone.sunk | while | flops 684197888 | bytes 35539192 | solution.py:113
  978.5 30.0 %while.58 = (s32[]{:T(128)}, f32[2048,64]{0,1:T(8,128)S(1)}, f32[2048,64]{0,1:T(8,128)S(1)}, f32[4,512,64]{1,2,0:T(8,128)}, s32[4]{0:T(128)S(1)}, /*index=5*/s32...) while((s32[]{:T(128)}, f32[2048,64]{0,1:T(8,128)S(1)}, ...), condition=%wide.region_15.15_spmd.clone, body=%wide.region_13.14_spmd.clone.sunk | while | flops 684197888 | bytes 35539192 | solution.py:113
  1017.1 30.0 %while.58 = (s32[]{:T(128)}, f32[2048,64]{0,1:T(8,128)S(1)}, f32[2048,64]{0,1:T(8,128)S(1)}, f32[4,512,64]{1,2,0:T(8,128)}, s32[4]{0:T(128)S(1)}, /*index=5*/s32...) while((s32[]{:T(128)}, f32[2048,64]{0,1:T(8,128)S(1)}, ...), condition=%wide.region_15.15_spmd.clone, body=%wide.region_13.14_spmd.clone.sunk | while | flops 684197888 | bytes 35539192 | solution.py:113
  1050.7 3.9 subtract_convert_fusion.1
  1062.3 7.1 bitcast_convert_fusion
  1070.7 7.4 fusion.52
  1079.5 6.9 convolution_convert_fusion
  1086.5 58.5 %reduce-scatter.18.cloned.1.call-done = bf16[512,1024]{1,0:T(8,128)(2,1)} async-done(((bf16[2048,1024]{1,0:T(8,128)(2,1)}), bf16[512,1024]{1,0:T(8,128)(2,1)}) %reduce-scatter.18.cloned.1.call-update) | async-done | bytes 1048592 | tf_op jit(solution)/shard_map/reduce_scatter | solution.py:228
  1144.9 2.0 fusion.47
  1148.1 7.8 fusion.68
  1156.0 11.5 fusion.39
  1168.7 4.4 fusion.67
  1173.2 3.0 copy.77
  1176.2 19.3 %reduce-scatter.20.cloned.1.call-done = f32[3,128,256]{1,2,0:T(8,128)} async-done(((f32[3,1024,256]{1,2,0:T(8,128)}), f32[3,128,256]{1,2,0:T(8,128)}) %reduce-scatter.20.cloned.1.call-update) | async-done | bytes 393232 | tf_op jit(solution)/shard_map/reduce_scatter | solution.py:242
  1195.5 1.9 copy.78
  1197.4 77.0 %reduce-scatter.14.cloned.1.call-done = bf16[512,1024]{1,0:T(8,128)(2,1)} async-done(((bf16[2048,1024]{1,0:T(8,128)(2,1)}), bf16[512,1024]{1,0:T(8,128)(2,1)}) %reduce-scatter.14.cloned.1.call-update) | async-done | bytes 1048592 | tf_op jit(solution)/shard_map/reduce_scatter | solution.py:176
  1274.5 4.3 fusion.44
  1278.7 33.8 %reduce-scatter.28.cloned.1.call-done = f32[128,2]{1,0:T(8,128)} async-done(((f32[1024,2]{1,0:T(8,128)}), f32[128,2]{1,0:T(8,128)}) %reduce-scatter.28.cloned.1.call-update) | async-done | bytes 1040
  1313.4 12.2 psum.7
  1325.6 35.6 %reduce-scatter.26.cloned.1.call-done = f32[704,128]{1,0:T(8,128)} async-done(((f32[704,1024]{1,0:T(8,128)}), f32[704,128]{1,0:T(8,128)}) %reduce-scatter.26.cloned.1.call-update) | async-done | bytes 360464 | tf_op jit(solution)/shard_map/reduce_scatter | solution.py:245
  1361.2 63.3 %reduce-scatter.24.cloned.1.call-done = f32[2,128,704]{1,2,0:T(8,128)} async-done(((f32[2,1024,704]{1,2,0:T(8,128)}), f32[2,128,704]{1,2,0:T(8,128)}) %reduce-scatter.24.cloned.1.call-update) | async-done | bytes 720912 | tf_op jit(solution)/shard_map/reduce_scatter | solution.py:244
  1424.5 39.6 %reduce-scatter.22.cloned.1.call-done = f32[256,128]{1,0:T(8,128)} async-done(((f32[256,1024]{1,0:T(8,128)}), f32[256,128]{1,0:T(8,128)}) %reduce-scatter.22.cloned.1.call-update) | async-done | bytes 131088 | tf_op jit(solution)/shard_map/reduce_scatter | solution.py:243
  (529 shorter events, 262.1 us)
Async XLA Ops:
  7.2 15.1 %copy-start.2 = (bf16[512,1024]{1,0:T(8,128)(2,1)S(1)}, bf16[512,1024]{1,0:T(8,128)(2,1)}, u32[]{:S(2)}) copy-start(bf16[512,1024]{1,0:T(8,128)(2,1)} %param.17) | copy-start | bytes 3145732
  7.2 32.6 %all-gather.10.cloned.1.call-start = ((), (), s32[]{:S(2)}) async-start(), calls=%async_computation.10 | async-start | bytes 1769472 | tf_op jit(solution)/shard_map/all_gather | solution.py:135
  9.1 113.8 %all-gather.8.cloned.1.call-start = ((), (), s32[]{:S(2)}) async-start(), calls=%async_computation.9 | async-start | bytes 5242880 | tf_op jit(solution)/shard_map/all_gather | solution.py:146
  20.1 4.3 copy-start.18
  20.1 4.3 copy-start.12
  21.7 2.6 copy-start.25
  22.3 2.0 copy-start.21
  23.6 389.0 %reduce-scatter.12.cloned.1.call-start = ((), (), s32[]{:S(2)}) async-start(), calls=%async_computation.11 | async-start | bytes 10485760 | tf_op jit(solution)/shard_map/reduce_scatter | solution.py:160
  38.8 90.7 %copy-start.8 = (f32[2048,32]{0,1:T(8,128)}, f32[2048,32]{0,1:T(8,128)S(1)}, u32[]{:S(2)}) copy-start(f32[2048,32]{0,1:T(8,128)S(1)} %get-tuple-element.429) | copy-start | bytes 786436
  262.7 6.7 copy-start.5
  269.4 1.1 copy-start.16
  269.4 143.2 %copy-start.3 = (bf16[512,1024]{1,0:T(8,128)(2,1)S(1)}, bf16[512,1024]{1,0:T(8,128)(2,1)}, u32[]{:S(2)}) copy-start(bf16[512,1024]{1,0:T(8,128)(2,1)} %param.17) | copy-start | bytes 3145732
  269.4 177.9 %all-gather.14.cloned.1.call-start = ((), (), s32[]{:S(2)}) async-start(), calls=%async_computation.13 | async-start | bytes 3244032 | tf_op jit(solution)/shard_map/all_gather | solution.py:137
  271.3 143.2 %copy-start.19 = (f32[1,1024]{1,0:T(1,128)S(1)}, f32[1,1024]{1,0:T(1,128)}, u32[]{:S(2)}) copy-start(f32[1,1024]{1,0:T(1,128)} %get-tuple-element.425) | copy-start | bytes 12292
  271.3 258.8 %all-gather.12.cloned.1.call-start = ((), (), s32[]{:S(2)}) async-start(), calls=%async_computation.12 | async-start | bytes 5242880 | tf_op jit(solution)/shard_map/all_gather | solution.py:168
  414.5 393.0 %copy-start = (f32[512,1024]{1,0:T(8,128)}, f32[512,1024]{1,0:T(8,128)S(1)}, u32[]{:S(2)}) copy-start(f32[512,1024]{1,0:T(8,128)S(1)} %get-tuple-element.395) | copy-start | bytes 6291460
  414.5 393.0 %copy-start.23 = (f32[512]{0:T(512)}, f32[512]{0:T(512)S(1)}, u32[]{:S(2)}) copy-start(f32[512]{0:T(512)S(1)} %add_rsqrt_fusion) | copy-start | bytes 6148
  414.6 1.3 copy-start.17
  415.8 140.4 %all-gather.16.cloned.1.call-start = ((), (), s32[]{:S(2)}) async-start(), calls=%async_computation.14 | async-start | bytes 1622016 | tf_op jit(solution)/shard_map/all_gather | solution.py:138
  416.6 222.0 %all-gather.18.cloned.1.call-start = ((), (), s32[]{:S(2)}) async-start(), calls=%async_computation.16 | async-start | bytes 5242880 | tf_op jit(solution)/shard_map/all_gather | solution.py:191
  417.3 387.3 %reduce-scatter.16.cloned.1.call-start = ((), (), s32[]{:S(2)}) async-start(), calls=%async_computation.17 | async-start | bytes 10485760 | tf_op jit(solution)/shard_map/reduce_scatter | solution.py:199
  638.6 13.9 copy-start.30
  649.9 1.5 copy-start.32
  649.9 2.5 copy-start.33
  661.5 146.1 %copy-start.7 = (bf16[512,1024]{1,0:T(8,128)(2,1)S(1)}, bf16[512,1024]{1,0:T(8,128)(2,1)}, u32[]{:S(2)}) copy-start(bf16[512,1024]{1,0:T(8,128)(2,1)} %param.25) | copy-start | bytes 3145732
  661.5 229.4 %all-gather.20.cloned.1.call-start = ((), (), s32[]{:S(2)}) async-start(), calls=%async_computation.18 | async-start | bytes 5242880 | tf_op jit(solution)/shard_map/all_gather | solution.py:210
  804.6 2.9 copy-start.6
  807.6 1.6 copy-start.27
  809.2 335.7 %reduce-scatter.18.cloned.1.call-start = ((), (), s32[]{:S(2)}) async-start(), calls=%async_computation.19 | async-start | bytes 5242880 | tf_op jit(solution)/shard_map/reduce_scatter | solution.py:228
  896.3 154.5 %copy-start.9 = (f32[2048,32]{0,1:T(8,128)S(1)}, f32[2048,32]{0,1:T(8,128)}, u32[]{:S(2)}) copy-start(f32[2048,32]{0,1:T(8,128)} %copy-done.8) | copy-start | bytes 786436
  1056.0 2.8 copy-start.10
  1060.4 1.3 copy-start.13
  1060.4 1.9 copy-start.14
  1069.5 1.2 copy-start.15
  1069.5 126.0 %reduce-scatter.20.cloned.1.call-start = ((), (), s32[]{:S(2)}) async-start(), calls=%async_computation.20 | async-start | bytes 3538944 | tf_op jit(solution)/shard_map/reduce_scatter | solution.py:242
  1078.1 1.4 copy-start.31
  1078.2 196.3 %reduce-scatter.14.cloned.1.call-start = ((), (), s32[]{:S(2)}) async-start(), calls=%async_computation.15 | async-start | bytes 5242880 | tf_op jit(solution)/shard_map/reduce_scatter | solution.py:176
  1086.4 58.5 %copy-start.4 = (bf16[512,1024]{1,0:T(8,128)(2,1)S(1)}, bf16[512,1024]{1,0:T(8,128)(2,1)}, u32[]{:S(2)}) copy-start(bf16[512,1024]{1,0:T(8,128)(2,1)} %param.17) | copy-start | bytes 3145732
  1086.4 58.5 %copy-start.22 = (f32[1,1024]{1,0:T(1,128)S(1)}, f32[1,1024]{1,0:T(1,128)}, u32[]{:S(2)}) copy-start(f32[1,1024]{1,0:T(1,128)} %copy-done.21) | copy-start | bytes 12292
  1086.4 58.5 %copy-start.26 = (f32[512]{0:T(512)S(1)}, f32[512]{0:T(512)}, u32[]{:S(2)}) copy-start(f32[512]{0:T(512)} %copy-done.25) | copy-start | bytes 6148
  1086.4 60.6 %copy-start.29 = (f32[1024]{0:T(1024)S(1)}, f32[1024]{0:T(1024)}, u32[]{:S(2)}) copy-start(f32[1024]{0:T(1024)} %get-tuple-element.318) | copy-start | bytes 12292
  1086.4 226.1 %reduce-scatter.28.cloned.1.call-start = ((), (), s32[]{:S(2)}) async-start(), calls=%async_computation.24 | async-start | bytes 589824
  1148.1 213.1 %reduce-scatter.26.cloned.1.call-start = ((), (), s32[]{:S(2)}) async-start(), calls=%async_computation.23 | async-start | bytes 3244032 | tf_op jit(solution)/shard_map/reduce_scatter | solution.py:245
  1155.9 268.6 %reduce-scatter.24.cloned.1.call-start = ((), (), s32[]{:S(2)}) async-start(), calls=%async_computation.22 | async-start | bytes 6488064 | tf_op jit(solution)/shard_map/reduce_scatter | solution.py:244
  1167.5 1.2 copy-start.11
  1167.5 296.6 %reduce-scatter.22.cloned.1.call-start = ((), (), s32[]{:S(2)}) async-start(), calls=%async_computation.21 | async-start | bytes 1179648 | tf_op jit(solution)/shard_map/reduce_scatter | solution.py:243
  1173.2 101.3 %copy-start.1 = (f32[512,1024]{1,0:T(8,128)S(1)}, f32[512,1024]{1,0:T(8,128)}, u32[]{:S(2)}) copy-start(f32[512,1024]{1,0:T(8,128)} %copy-done) | copy-start | bytes 6291460
  1173.2 101.3 %copy-start.20 = (f32[1,1024]{1,0:T(1,128)S(1)}, f32[1,1024]{1,0:T(1,128)}, u32[]{:S(2)}) copy-start(f32[1,1024]{1,0:T(1,128)} %get-tuple-element.425) | copy-start | bytes 12292
  1173.2 101.3 %copy-start.24 = (f32[512]{0:T(512)S(1)}, f32[512]{0:T(512)}, u32[]{:S(2)}) copy-start(f32[512]{0:T(512)} %copy-done.23) | copy-start | bytes 6148
  1173.2 101.2 %copy-start.28 = (f32[512]{0:T(512)S(1)}, f32[512]{0:T(512)}, u32[]{:S(2)}) copy-start(f32[512]{0:T(512)} %copy-done.27) | copy-start | bytes 6148
Sparse Core Ops, SparseCore 0:
  10.5 29.2 all-gather.9
  41.9 80.9 all-gather.7
  269.5 143.0 reduce-scatter.11
  414.9 32.3 all-gather.13
  449.3 80.7 all-gather.11
  532.4 23.8 all-gather.15
  557.8 80.7 all-gather.17
  661.6 143.0 reduce-scatter.15
  809.4 81.4 all-gather.19
  1069.6 75.2 reduce-scatter.17
  1148.7 46.7 reduce-scatter.19
  1197.7 76.7 reduce-scatter.13
  1277.8 34.6 reduce-scatter.27
  1316.3 44.8 reduce-scatter.25
  1365.5 58.9 reduce-scatter.23
  1428.1 35.9 reduce-scatter.21
where the time goes:
time: 1480 us; the launch traced here: 1470 us
  waiting for transfers between devices  987 us (67%)
  matrix products  226 us (15%)
  local copies, waits for them, and re-layouts  102 us (7%)
  other arithmetic  81.1 us (5%)
  blocking collectives  34.4 us (2%)
  loops' own time  22.6 us (2%)
  between operations  15.4 us (1%)
    reduce_scatter x1, waiting for transfers between devices, shards(): lax.psum_scatter(jnp.einsum('ktf,kdf->td', piece, gates_back, preferred_e...  143 us
    reduce_scatter x1, waiting for transfers between devices, shards(): lax.psum_scatter(jnp.dot(piece, proj_full, preferred_element_type=jnp.flo...  141 us
    all_gather x1, waiting for transfers between devices, shards(): lax.all_gather(normed_a.astype(jnp.bfloat16), 'head', axis=0, tiled=True)  83.2 us
    all_gather x1, waiting for transfers between devices, shards(): lax.all_gather(normed_b.astype(jnp.bfloat16), 'head', axis=0, tiled=True)  82.8 us
    all_gather x1, waiting for transfers between devices, shards(): piece = lax.all_gather(cotangent, 'head', axis=0, tiled=True)  82.4 us
    all_gather x1, waiting for transfers between devices, shards(): piece = lax.all_gather(branch_grad, 'head', axis=0, tiled=True)  81.4 us
    reduce_scatter x1, waiting for transfers between devices, shards(): lax.psum_scatter(jnp.dot(piece, down_full, preferred_element_type=jnp.flo...  77 us
    reduce_scatter x1, waiting for transfers between devices, shards(): lax.psum_scatter(gates_part, 'dp', scatter_dimension=1, tiled=True)  63.3 us
  transfers between devices with their start and end apart: 16, of which 16 were waited for; matrix products, arithmetic and copies ran while one was open for 5% of the time, Pallas kernels for 0%

commit v1 on v0

--- a/solution.py
+++ b/solution.py
@@ -8,6 +8,27 @@
 epsilon = 1e-05
 far_below = -1e30
 rope_base = 10000.0
+
+
+def collect(x, axis, dim):
+    devices, index, width = (lax.axis_size(axis), lax.axis_index(axis), x.shape[dim])
+    forward = [(i, (i + 1) % devices) for i in range(devices)]
+    backward = [(i, (i - 1) % devices) for i in range(devices)]
+    whole = jnp.zeros((*x.shape[:dim], devices * width, *x.shape[dim + 1 :]), x.dtype)
+    whole = lax.dynamic_update_slice_in_dim(whole, x, index * width, axis=dim)
+    from_left = from_right = x
+    half = devices // 2
+    for turn in range(1, half + 1):
+        from_left = lax.ppermute(from_left, axis, forward)
+        whole = lax.dynamic_update_slice_in_dim(
+            whole, from_left, (index - turn) % devices * width, axis=dim
+        )
+        if turn < devices - half:
+            from_right = lax.ppermute(from_right, axis, backward)
+            whole = lax.dynamic_update_slice_in_dim(
+                whole, from_right, (index + turn) % devices * width, axis=dim
+            )
+    return whole
 
 
 def rope_tables(width):
@@ -188,7 +209,7 @@
         lax.all_gather(gain_low, "dp", axis=1, tiled=True),
     )
     qkv_back, proj_back, gates_back, down_back, gain_back = back_full
-    piece = lax.all_gather(cotangent, "head", axis=0, tiled=True)
+    piece = collect(cotangent, "head", 0)
     down_sum = jnp.einsum("tf,td->fd", inner, piece, preferred_element_type=jnp.float32)
     rows_grad = jnp.einsum("td,fd->tf", piece, down_back, preferred_element_type=jnp.float32)
     inner_grad = rows_grad

time: 1480 us -> 1430 us (0.966)
  waiting for transfers between devices: 987 us -> 891 us
  starting transfers between devices: 1.82 us -> 31.1 us
    all_gather x1 -> x0, waiting for transfers between devices: 82.4 us -> none  [shards(): piece = lax.all_gather(cotangent, 'head', axis=0, tiled=True)]
    ppermute x0 -> x3, waiting for transfers between devices: none -> 60.1 us  [the longest x2 56.8 us: collect(): from_left = lax.ppermute(from_left, axis, forward)]
    all_gather x1, waiting for transfers between devices: 82.8 us -> 38.5 us  [shards(): lax.all_gather(normed_b.astype(jnp.bfloat16), 'head', axis=0, tiled=True)]
    ppermute x0 -> x3, starting transfers between devices: none -> 29.8 us  [the longest x2 26.6 us: collect(): from_left = lax.ppermute(from_left, axis, forward)]
    all_gather x1, waiting for transfers between devices: 29.4 us -> 0.01 us  [shards(): lax.all_gather(gates_low, 'dp', axis=1, tiled=True)]
    unnamed x17 -> x16, waiting for transfers between devices: 34.7 us -> 33.9 us
  transfers between devices with their start and end apart: 16 -> 18, of which waited for: 16 -> 16; matrix products, arithmetic and copies ran while one was open for 5% -> 6% of each run, Pallas kernels for 0% -> 0%
where the time goes in v1:
time: 1430 us; the launch traced here: 1420 us
  waiting for transfers between devices  891 us (62%)
  matrix products  227 us (16%)
  local copies, waits for them, and re-layouts  113 us (8%)
  other arithmetic  82.6 us (6%)
  blocking collectives  35.4 us (2%)
  starting transfers between devices  31.1 us (2%)
  loops' own time  22.5 us (2%)
  between operations  15.4 us (1%)
    reduce_scatter x1, waiting for transfers between devices, shards(): lax.psum_scatter(jnp.einsum('ktf,kdf->td', piece, gates_back, preferred_e...  145 us
    reduce_scatter x1, waiting for transfers between devices, shards(): lax.psum_scatter(jnp.dot(piece, proj_full, preferred_element_type=jnp.flo...  141 us
    all_gather x1, waiting for transfers between devices, shards(): lax.all_gather(normed_a.astype(jnp.bfloat16), 'head', axis=0, tiled=True)  81.9 us
    all_gather x1, waiting for transfers between devices, shards(): piece = lax.all_gather(branch_grad, 'head', axis=0, tiled=True)  81.4 us
    reduce_scatter x1, waiting for transfers between devices, shards(): lax.psum_scatter(jnp.dot(piece, down_full, preferred_element_type=jnp.flo...  77.2 us
    reduce_scatter x1, waiting for transfers between devices, shards(): lax.psum_scatter(gates_part, 'dp', scatter_dimension=1, tiled=True)  63.3 us
    dot_general x32, matrix products, block_scores(): jnp.einsum('qe,ke->qk', query_block, keys, preferred_element_type=jnp.flo...  61.9 us
    reduce_scatter x1, waiting for transfers between devices, shards(): lax.psum_scatter(jnp.einsum('ktc,kdc->td', piece, qkv_back, preferred_ele...  58.1 us
  transfers between devices with their start and end apart: 18, of which 16 were waited for; matrix products, arithmetic and copies ran while one was open for 6% of the time, Pallas kernels for 0%

profile of v1, /device:TPU:0, one launch (start us, length us, event | category | flops | bytes accessed | tf_op | source)
XLA Modules:
  0.0 1417.8 jit_solution(1695647114268749028)
XLA Ops:
  9.9 10.2 all_gather.29
  22.8 2.5 fusion.45
  26.7 13.0 all_gather.32
  41.6 81.9 %all-gather.7.cloned.1.call-done = bf16[2048,1024]{1,0:T(8,128)(2,1)} async-done(((bf16[512,1024]{1,0:T(8,128)(2,1)}), bf16[2048,1024]{1,0:T(8,128)(2,1)}) %all-gather.7.cloned.1.call-update) | async-done | bytes 4194320 | tf_op jit(solution)/shard_map/all_gather | solution.py:167
  123.4 5.7 fusion.29
  135.4 127.7 %while.54 = (s32[]{:T(128)}, bf16[4,2048,64]{1,2,0:T(8,128)(2,1)}, f32[4,2048]{1,0:T(4,128)S(1)}, bf16[4,2048,64]{2,1,0:T(8,128)(2,1)}, bf16[4,2048,64]{2,1,0:T(...) while((s32[]{:T(128)}, bf16[4,2048,64]{1,2,0:T(8,128)(2,1)}, ...), condition=%wide.region_6.7_spmd, body=%wide.region_1.6_spmd.sunk | while | flops 278990336 | bytes 16777708 | solution.py:176
  139.0 27.0 %while.57 = (s32[]{:T(128)}, bf16[4,512,64]{1,2,0:T(8,128)(2,1)S(1)}, f32[4,512]{1,0:T(4,128)S(1)}, s32[4]{0:T(128)S(1)}, s32[]{:T(128)}, /*index=5*/bf16[2048,6...) while((s32[]{:T(128)}, ...), condition=%wide.region_5.5_spmd, body=%wide.region_2.4_spmd.sunk | while | flops 278990336 | bytes 13598931 | solution.py:104
  141.6 2.3 fusion.119
  148.3 2.3 fusion.119
  155.1 2.3 fusion.119
  161.8 2.3 fusion.119
  170.9 27.0 %while.57 = (s32[]{:T(128)}, bf16[4,512,64]{1,2,0:T(8,128)(2,1)S(1)}, f32[4,512]{1,0:T(4,128)S(1)}, s32[4]{0:T(128)S(1)}, s32[]{:T(128)}, /*index=5*/bf16[2048,6...) while((s32[]{:T(128)}, ...), condition=%wide.region_5.5_spmd, body=%wide.region_2.4_spmd.sunk | while | flops 278990336 | bytes 13598931 | solution.py:104
  173.5 2.3 fusion.119
  180.3 2.3 fusion.119
  187.0 2.3 fusion.119
  193.7 2.3 fusion.119
  202.8 27.0 %while.57 = (s32[]{:T(128)}, bf16[4,512,64]{1,2,0:T(8,128)(2,1)S(1)}, f32[4,512]{1,0:T(4,128)S(1)}, s32[4]{0:T(128)S(1)}, s32[]{:T(128)}, /*index=5*/bf16[2048,6...) while((s32[]{:T(128)}, ...), condition=%wide.region_5.5_spmd, body=%wide.region_2.4_spmd.sunk | while | flops 278990336 | bytes 13598931 | solution.py:104
  205.4 2.3 fusion.119
  212.2 2.3 fusion.119
  218.9 2.3 fusion.119
  225.7 2.3 fusion.119
  234.8 27.0 %while.57 = (s32[]{:T(128)}, bf16[4,512,64]{1,2,0:T(8,128)(2,1)S(1)}, f32[4,512]{1,0:T(4,128)S(1)}, s32[4]{0:T(128)S(1)}, s32[]{:T(128)}, /*index=5*/bf16[2048,6...) while((s32[]{:T(128)}, ...), condition=%wide.region_5.5_spmd, body=%wide.region_2.4_spmd.sunk | while | flops 278990336 | bytes 13598931 | solution.py:104
  237.4 2.3 fusion.119
  244.1 2.3 fusion.119
  250.8 2.3 fusion.119
  263.1 6.7 fusion.66
  271.8 141.2 %reduce-scatter.12.cloned.1.call-done = f32[512,1024]{1,0:T(8,128)} async-done(((f32[2048,1024]{1,0:T(8,128)}), f32[512,1024]{1,0:T(8,128)}) %reduce-scatter.12.cloned.1.call-update) | async-done | bytes 2097168 | tf_op jit(solution)/shard_map/reduce_scatter | solution.py:181
  418.1 3.2 collective-permute-start.1
  422.1 22.9 %collective-permute-done = bf16[512,1024]{1,0:T(8,128)(2,1)} collective-permute-done((bf16[512,1024]{1,0:T(8,128)(2,1)S(1)}, bf16[512,1024]{1,0:T(8,128)(2,1)}, u32[]{:S(2)}, u32[]{:S(2)}) %collective-permute-start) | collective-permute-done | bytes 1048608 | tf_op jit(solution)/shard_map/ppermute | solution.py:22
  445.0 25.5 %collective-permute-start.2 = (bf16[512,1024]{1,0:T(8,128)(2,1)}, bf16[512,1024]{1,0:T(8,128)(2,1)}, u32[]{:S(2)}, u32[]{:S(2)}) collective-permute-start(bf16[512,1024]{1,0:T(8,128)(2,1)} %collective-permute-done), channel_id=1, source_target_pairs={{0,1},{1,2},{2,3},{3,0},{4,5},{5,6},{6,7},{7,4},{8,9},{9,10},{10,1... | collective-permute-start | bytes 3145736 | tf_op jit(solution)/shard_map/ppermute | solution.py:22
  470.4 2.5 broadcast_in_dim.70
  476.2 3.3 collective-permute-done.1
  481.8 33.9 %collective-permute-done.2 = bf16[512,1024]{1,0:T(8,128)(2,1)} collective-permute-done((bf16[512,1024]{1,0:T(8,128)(2,1)}, bf16[512,1024]{1,0:T(8,128)(2,1)}, u32[]{:S(2)}, u32[]{:S(2)}) %collective-permute-start.2) | collective-permute-done | bytes 1048608 | tf_op jit(solution)/shard_map/ppermute | solution.py:22
  518.0 38.5 %all-gather.11.cloned.1.call-done = bf16[2048,1024]{1,0:T(8,128)(2,1)} async-done(((bf16[512,1024]{1,0:T(8,128)(2,1)}), bf16[2048,1024]{1,0:T(8,128)(2,1)}) %all-gather.11.cloned.1.call-update) | async-done | bytes 4194320 | tf_op jit(solution)/shard_map/all_gather | solution.py:189
  556.5 11.5 convolution_bitcast_fusion.1
  567.9 16.0 %all-gather.15.cloned.1.call-done = bf16[704,1024]{1,0:T(8,128)(2,1)} async-done(((bf16[704,128]{1,0:T(8,128)(2,1)}), bf16[704,1024]{1,0:T(8,128)(2,1)}) %all-gather.15.cloned.1.call-update) | async-done | bytes 1441808 | tf_op jit(solution)/shard_map/all_gather | solution.py:159
  583.9 11.3 fusion.37
  597.8 9.0 convolution_bitcast_fusion.2
  606.9 144.6 %reduce-scatter.16.cloned.1.call-done = f32[512,1024]{1,0:T(8,128)} async-done(((f32[2048,1024]{1,0:T(8,128)}), f32[512,1024]{1,0:T(8,128)}) %reduce-scatter.16.cloned.1.call-update) | async-done | bytes 2097168 | tf_op jit(solution)/shard_map/reduce_scatter | solution.py:220
  751.5 2.9 multiply_reduce_fusion.1
  756.3 81.4 %all-gather.17.cloned.1.call-done = bf16[2048,1024]{1,0:T(8,128)(2,1)} async-done(((bf16[512,1024]{1,0:T(8,128)(2,1)}), bf16[2048,1024]{1,0:T(8,128)(2,1)}) %all-gather.17.cloned.1.call-update) | async-done | bytes 4194320 | tf_op jit(solution)/shard_map/all_gather | solution.py:231
  837.7 3.6 fusion.38
  843.1 155.5 %while.56 = (s32[]{:T(128)}, f32[4,2048,64]{1,2,0:T(8,128)}, f32[4,2048,64]{1,2,0:T(8,128)}, f32[4,2048,64]{1,2,0:T(8,128)}, bf16[4,2048,64]{2,1,0:T(8,128)(2,1)...) while((s32[]{:T(128)}, f32[4,2048,64]{1,2,0:T(8,128)}, ...), condition=%wide.region_16.17_spmd, body=%wide.region_12.16_spmd.sunk | while | flops 684197888 | bytes 42895948 | solution.py:237
  848.1 30.3 %while.58 = (s32[]{:T(128)}, f32[2048,64]{0,1:T(8,128)S(1)}, f32[2048,64]{0,1:T(8,128)S(1)}, f32[4,512,64]{1,2,0:T(8,128)}, s32[4]{0:T(128)S(1)}, /*index=5*/s32...) while((s32[]{:T(128)}, f32[2048,64]{0,1:T(8,128)S(1)}, ...), condition=%wide.region_15.15_spmd.clone, body=%wide.region_13.14_spmd.clone.sunk | while | flops 684197888 | bytes 35539192 | solution.py:134
  887.0 30.3 %while.58 = (s32[]{:T(128)}, f32[2048,64]{0,1:T(8,128)S(1)}, f32[2048,64]{0,1:T(8,128)S(1)}, f32[4,512,64]{1,2,0:T(8,128)}, s32[4]{0:T(128)S(1)}, /*index=5*/s32...) while((s32[]{:T(128)}, f32[2048,64]{0,1:T(8,128)S(1)}, ...), condition=%wide.region_15.15_spmd.clone, body=%wide.region_13.14_spmd.clone.sunk | while | flops 684197888 | bytes 35539192 | solution.py:134
  925.9 30.3 %while.58 = (s32[]{:T(128)}, f32[2048,64]{0,1:T(8,128)S(1)}, f32[2048,64]{0,1:T(8,128)S(1)}, f32[4,512,64]{1,2,0:T(8,128)}, s32[4]{0:T(128)S(1)}, /*index=5*/s32...) while((s32[]{:T(128)}, f32[2048,64]{0,1:T(8,128)S(1)}, ...), condition=%wide.region_15.15_spmd.clone, body=%wide.region_13.14_spmd.clone.sunk | while | flops 684197888 | bytes 35539192 | solution.py:134
  964.8 30.3 %while.58 = (s32[]{:T(128)}, f32[2048,64]{0,1:T(8,128)S(1)}, f32[2048,64]{0,1:T(8,128)S(1)}, f32[4,512,64]{1,2,0:T(8,128)}, s32[4]{0:T(128)S(1)}, /*index=5*/s32...) while((s32[]{:T(128)}, f32[2048,64]{0,1:T(8,128)S(1)}, ...), condition=%wide.region_15.15_spmd.clone, body=%wide.region_13.14_spmd.clone.sunk | while | flops 684197888 | bytes 35539192 | solution.py:134
  998.6 3.8 subtract_convert_fusion.1
  1008.7 7.5 bitcast_convert_fusion
  1017.7 7.4 fusion.52
  1026.5 6.9 convolution_convert_fusion
  1033.5 58.1 %reduce-scatter.18.cloned.1.call-done = bf16[512,1024]{1,0:T(8,128)(2,1)} async-done(((bf16[2048,1024]{1,0:T(8,128)(2,1)}), bf16[512,1024]{1,0:T(8,128)(2,1)}) %reduce-scatter.18.cloned.1.call-update) | async-done | bytes 1048592 | tf_op jit(solution)/shard_map/reduce_scatter | solution.py:249
  1094.8 7.7 fusion.68
  1102.6 11.5 fusion.39
  1115.4 4.5 fusion.67
  1119.9 3.0 copy.77
  1122.9 19.1 %reduce-scatter.20.cloned.1.call-done = f32[3,128,256]{1,2,0:T(8,128)} async-done(((f32[3,1024,256]{1,2,0:T(8,128)}), f32[3,128,256]{1,2,0:T(8,128)}) %reduce-scatter.20.cloned.1.call-update) | async-done | bytes 393232 | tf_op jit(solution)/shard_map/reduce_scatter | solution.py:263
  1143.9 77.2 %reduce-scatter.14.cloned.1.call-done = bf16[512,1024]{1,0:T(8,128)(2,1)} async-done(((bf16[2048,1024]{1,0:T(8,128)(2,1)}), bf16[512,1024]{1,0:T(8,128)(2,1)}) %reduce-scatter.14.cloned.1.call-update) | async-done | bytes 1048592 | tf_op jit(solution)/shard_map/reduce_scatter | solution.py:197
  1221.1 4.3 fusion.44
  1225.4 33.7 %reduce-scatter.28.cloned.1.call-done = f32[128,2]{1,0:T(8,128)} async-done(((f32[1024,2]{1,0:T(8,128)}), f32[128,2]{1,0:T(8,128)}) %reduce-scatter.28.cloned.1.call-update) | async-done | bytes 1040
  1259.9 12.2 psum.7
  1272.2 35.7 %reduce-scatter.26.cloned.1.call-done = f32[704,128]{1,0:T(8,128)} async-done(((f32[704,1024]{1,0:T(8,128)}), f32[704,128]{1,0:T(8,128)}) %reduce-scatter.26.cloned.1.call-update) | async-done | bytes 360464 | tf_op jit(solution)/shard_map/reduce_scatter | solution.py:266
  1307.9 63.3 %reduce-scatter.24.cloned.1.call-done = f32[2,128,704]{1,2,0:T(8,128)} async-done(((f32[2,1024,704]{1,2,0:T(8,128)}), f32[2,128,704]{1,2,0:T(8,128)}) %reduce-scatter.24.cloned.1.call-update) | async-done | bytes 720912 | tf_op jit(solution)/shard_map/reduce_scatter | solution.py:265
  1371.2 39.6 %reduce-scatter.22.cloned.1.call-done = f32[256,128]{1,0:T(8,128)} async-done(((f32[256,1024]{1,0:T(8,128)}), f32[256,128]{1,0:T(8,128)}) %reduce-scatter.22.cloned.1.call-update) | async-done | bytes 131088 | tf_op jit(solution)/shard_map/reduce_scatter | solution.py:264
  (533 shorter events, 278.8 us)
Async XLA Ops:
  7.2 18.9 %copy-start.16 = (f32[256,128]{1,0:T(8,128)S(1)}, f32[256,128]{1,0:T(8,128)}, u32[]{:S(2)}) copy-start(f32[256,128]{1,0:T(8,128)} %param.20) | copy-start | bytes 393220
  7.2 18.9 %copy-start.11 = (bf16[2048,256]{1,0:T(8,128)(2,1)S(1)}, bf16[2048,256]{1,0:T(8,128)(2,1)}, u32[]{:S(2)}) copy-start(bf16[2048,256]{1,0:T(8,128)(2,1)} %param.18) | copy-start | bytes 3145732
  7.2 34.4 %all-gather.9.cloned.1.call-start = ((), (), s32[]{:S(2)}) async-start(), calls=%async_computation.10 | async-start | bytes 1769472 | tf_op jit(solution)/shard_map/all_gather | solution.py:156
  9.2 114.3 %all-gather.7.cloned.1.call-start = ((), (), s32[]{:S(2)}) async-start(), calls=%async_computation.9 | async-start | bytes 5242880 | tf_op jit(solution)/shard_map/all_gather | solution.py:167
  21.6 0.6 copy-start.23
  22.2 0.6 copy-start.19
  25.3 387.7 %reduce-scatter.12.cloned.1.call-start = ((), (), s32[]{:S(2)}) async-start(), calls=%async_computation.11 | async-start | bytes 10485760 | tf_op jit(solution)/shard_map/reduce_scatter | solution.py:181
  41.5 88.4 %copy-start.7 = (f32[2048,32]{0,1:T(8,128)}, f32[2048,32]{0,1:T(8,128)S(1)}, u32[]{:S(2)}) copy-start(f32[2048,32]{0,1:T(8,128)S(1)} %get-tuple-element.429) | copy-start | bytes 786436
  263.1 6.7 copy-start.4
  269.8 1.1 copy-start.14
  269.8 143.2 %copy-start.2 = (bf16[512,1024]{1,0:T(8,128)(2,1)S(1)}, bf16[512,1024]{1,0:T(8,128)(2,1)}, u32[]{:S(2)}) copy-start(bf16[512,1024]{1,0:T(8,128)(2,1)} %param.17) | copy-start | bytes 3145732
  269.8 248.2 %all-gather.13.cloned.1.call-start = ((), (), s32[]{:S(2)}) async-start(), calls=%async_computation.13 | async-start | bytes 3244032 | tf_op jit(solution)/shard_map/all_gather | solution.py:158
  271.7 143.3 %copy-start.17 = (f32[1,1024]{1,0:T(1,128)S(1)}, f32[1,1024]{1,0:T(1,128)}, u32[]{:S(2)}) copy-start(f32[1,1024]{1,0:T(1,128)} %get-tuple-element.425) | copy-start | bytes 12292
  271.7 284.7 %all-gather.11.cloned.1.call-start = ((), (), s32[]{:S(2)}) async-start(), calls=%async_computation.12 | async-start | bytes 5242880 | tf_op jit(solution)/shard_map/all_gather | solution.py:189
  414.9 339.5 %copy-start = (f32[512,1024]{1,0:T(8,128)}, f32[512,1024]{1,0:T(8,128)S(1)}, u32[]{:S(2)}) copy-start(f32[512,1024]{1,0:T(8,128)S(1)} %get-tuple-element.395) | copy-start | bytes 6291460
  414.9 2.0 copy-start.6
  414.9 6.4 copy-start.15
  415.0 339.4 %copy-start.21 = (f32[512]{0:T(512)}, f32[512]{0:T(512)S(1)}, u32[]{:S(2)}) copy-start(f32[512]{0:T(512)S(1)} %add_rsqrt_fusion) | copy-start | bytes 6148
  416.2 167.7 %all-gather.15.cloned.1.call-start = ((), (), s32[]{:S(2)}) async-start(), calls=%async_computation.14 | async-start | bytes 1622016 | tf_op jit(solution)/shard_map/all_gather | solution.py:159
  416.9 28.0 %collective-permute-start = (bf16[512,1024]{1,0:T(8,128)(2,1)S(1)}, bf16[512,1024]{1,0:T(8,128)(2,1)}, u32[]{:S(2)}, u32[]{:S(2)}) collective-permute-start(bf16[512,1024]{1,0:T(8,128)(2,1)S(1)} %copy-done.6), channel_id=1, source_target_pairs={{0,1},{1,2},{2,3},{3,0},{4,5},{5,6},{6,7},{7,4},{8,9},{9,10},{10,1... | collective-permute-start | bytes 3145736 | tf_op jit(solution)/shard_map/ppermute | solution.py:22
  418.1 61.4 %collective-permute-start.1 = (bf16[512,1024]{1,0:T(8,128)(2,1)S(1)}, bf16[512,1024]{1,0:T(8,128)(2,1)}, u32[]{:S(2)}, u32[]{:S(2)}) collective-permute-start(bf16[512,1024]{1,0:T(8,128)(2,1)S(1)} %copy-done.6), channel_id=1, source_target_pairs={{0,3},{1,0},{2,1},{3,2},{4,7},{5,4},{6,5},{7,6},{8,11},{9,8},{10,9... | collective-permute-start | bytes 3145736 | tf_op jit(solution)/shard_map/ppermute | solution.py:27
  422.0 329.4 %reduce-scatter.16.cloned.1.call-start = ((), (), s32[]{:S(2)}) async-start(), calls=%async_computation.16 | async-start | bytes 10485760 | tf_op jit(solution)/shard_map/reduce_scatter | solution.py:220
  445.0 70.8 %collective-permute-start.2 = (bf16[512,1024]{1,0:T(8,128)(2,1)}, bf16[512,1024]{1,0:T(8,128)(2,1)}, u32[]{:S(2)}, u32[]{:S(2)}) collective-permute-start(bf16[512,1024]{1,0:T(8,128)(2,1)} %collective-permute-done), channel_id=1, source_target_pairs={{0,1},{1,2},{2,3},{3,0},{4,5},{5,6},{6,7},{7,4},{8,9},{9,10},{10,1... | collective-permute-start | bytes 3145736 | tf_op jit(solution)/shard_map/ppermute | solution.py:22
  583.9 13.9 copy-start.28
  595.3 1.5 copy-start.30
  595.3 2.6 copy-start.31
  606.8 230.8 %all-gather.17.cloned.1.call-start = ((), (), s32[]{:S(2)}) async-start(), calls=%async_computation.17 | async-start | bytes 5242880 | tf_op jit(solution)/shard_map/all_gather | solution.py:231
  751.5 2.9 copy-start.5
  754.4 1.6 copy-start.25
  756.0 335.5 %reduce-scatter.18.cloned.1.call-start = ((), (), s32[]{:S(2)}) async-start(), calls=%async_computation.18 | async-start | bytes 5242880 | tf_op jit(solution)/shard_map/reduce_scatter | solution.py:249
  843.1 155.5 %copy-start.8 = (f32[2048,32]{0,1:T(8,128)S(1)}, f32[2048,32]{0,1:T(8,128)}, u32[]{:S(2)}) copy-start(f32[2048,32]{0,1:T(8,128)} %copy-done.7) | copy-start | bytes 786436
  1002.6 3.9 copy-start.9
  1016.1 1.2 copy-start.12
  1016.1 1.5 copy-start.13
  1016.2 125.9 %reduce-scatter.20.cloned.1.call-start = ((), (), s32[]{:S(2)}) async-start(), calls=%async_computation.19 | async-start | bytes 3538944 | tf_op jit(solution)/shard_map/reduce_scatter | solution.py:263
  1025.1 1.4 copy-start.29
  1025.1 196.0 %reduce-scatter.14.cloned.1.call-start = ((), (), s32[]{:S(2)}) async-start(), calls=%async_computation.15 | async-start | bytes 5242880 | tf_op jit(solution)/shard_map/reduce_scatter | solution.py:197
  1033.4 58.2 %copy-start.3 = (bf16[512,1024]{1,0:T(8,128)(2,1)S(1)}, bf16[512,1024]{1,0:T(8,128)(2,1)}, u32[]{:S(2)}) copy-start(bf16[512,1024]{1,0:T(8,128)(2,1)} %param.17) | copy-start | bytes 3145732
  1033.4 58.2 %copy-start.20 = (f32[1,1024]{1,0:T(1,128)S(1)}, f32[1,1024]{1,0:T(1,128)}, u32[]{:S(2)}) copy-start(f32[1,1024]{1,0:T(1,128)} %copy-done.19) | copy-start | bytes 12292
  1033.4 58.2 %copy-start.24 = (f32[512]{0:T(512)S(1)}, f32[512]{0:T(512)}, u32[]{:S(2)}) copy-start(f32[512]{0:T(512)} %copy-done.23) | copy-start | bytes 6148
  1033.4 60.2 %copy-start.27 = (f32[1024]{0:T(1024)S(1)}, f32[1024]{0:T(1024)}, u32[]{:S(2)}) copy-start(f32[1024]{0:T(1024)} %get-tuple-element.318) | copy-start | bytes 12292
  1033.4 225.6 %reduce-scatter.28.cloned.1.call-start = ((), (), s32[]{:S(2)}) async-start(), calls=%async_computation.23 | async-start | bytes 589824
  1094.7 213.1 %reduce-scatter.26.cloned.1.call-start = ((), (), s32[]{:S(2)}) async-start(), calls=%async_computation.22 | async-start | bytes 3244032 | tf_op jit(solution)/shard_map/reduce_scatter | solution.py:266
  1102.6 268.7 %reduce-scatter.24.cloned.1.call-start = ((), (), s32[]{:S(2)}) async-start(), calls=%async_computation.21 | async-start | bytes 6488064 | tf_op jit(solution)/shard_map/reduce_scatter | solution.py:265
  1114.1 1.2 copy-start.10
  1114.2 296.7 %reduce-scatter.22.cloned.1.call-start = ((), (), s32[]{:S(2)}) async-start(), calls=%async_computation.20 | async-start | bytes 1179648 | tf_op jit(solution)/shard_map/reduce_scatter | solution.py:264
  1119.8 101.3 %copy-start.1 = (f32[512,1024]{1,0:T(8,128)S(1)}, f32[512,1024]{1,0:T(8,128)}, u32[]{:S(2)}) copy-start(f32[512,1024]{1,0:T(8,128)} %copy-done) | copy-start | bytes 6291460
  1119.9 101.3 %copy-start.18 = (f32[1,1024]{1,0:T(1,128)S(1)}, f32[1,1024]{1,0:T(1,128)}, u32[]{:S(2)}) copy-start(f32[1,1024]{1,0:T(1,128)} %get-tuple-element.425) | copy-start | bytes 12292
  1119.9 101.3 %copy-start.22 = (f32[512]{0:T(512)S(1)}, f32[512]{0:T(512)}, u32[]{:S(2)}) copy-start(f32[512]{0:T(512)} %copy-done.21) | copy-start | bytes 6148
  1119.9 101.3 %copy-start.26 = (f32[512]{0:T(512)S(1)}, f32[512]{0:T(512)}, u32[]{:S(2)}) copy-start(f32[512]{0:T(512)} %copy-done.25) | copy-start | bytes 6148
Sparse Core Ops, SparseCore 0:
  10.5 30.0 all-gather.8
  42.7 80.7 all-gather.6
  270.0 142.9 reduce-scatter.11
  415.3 32.3 all-gather.12
  449.7 106.7 all-gather.10
  558.8 25.1 all-gather.14
  607.0 144.4 reduce-scatter.15
  756.2 81.4 all-gather.16
  1016.3 75.2 reduce-scatter.17
  1095.2 46.7 reduce-scatter.19
  1144.3 76.7 reduce-scatter.13
  1224.3 34.6 reduce-scatter.27
  1263.0 44.8 reduce-scatter.25
  1312.2 59.0 reduce-scatter.23
  1374.8 35.9 reduce-scatter.21
